TPU v7x, 256 devices: a whole 4x4x8 slice. The times are simulated.
256 devices in a mesh: dp: 16 (over x, y_hi, core), expert: 16 (over z, y_lo).
Axes of the slice: x: 4, y: 4 (y_hi: 2, y_lo: 2; y = y_hi * 2 + y_lo), z: 8, core: 2. Of those that a mesh axis runs over, the one named last changes fastest.
Arguments:
- tokens: bfloat16 [2048, 4096], P('expert', 'dp'), may hold values from -6 to 6
- expert_ids: int32 [2048, 8], P('expert'), may hold values from 0 to 63, all different within a row; in each aligned block of 128 rows (0 to 127, 128 to 255, ...) at most 32 rows name the same one
- gate_prob: float32 [2048, 8], P('expert'), may hold values from 0.05 to 0.35
- w_gate: bfloat16 [64, 4096, 768], P('expert', 'dp'), may hold values from -0.09375 to 0.09375
- w_up: bfloat16 [64, 4096, 768], P('expert', 'dp'), may hold values from -0.09375 to 0.09375
- w_down: bfloat16 [64, 768, 4096], P('expert', None, 'dp'), may hold values from -0.21875 to 0.21875
- grad_out: bfloat16 [2048, 4096], P('expert', 'dp'), may hold values from -6 to 6
Outputs:
- mixed: bfloat16 [2048, 4096], P('expert', 'dp')
- grad_tokens: bfloat16 [2048, 4096], P('expert', 'dp')
- grad_gate: float32 [2048, 8], P('expert')
- grad_w_gate: bfloat16 [64, 4096, 768], P('expert', 'dp')
- grad_w_up: bfloat16 [64, 4096, 768], P('expert', 'dp')
- grad_w_down: bfloat16 [64, 768, 4096], P('expert', None, 'dp')
Inputs may be any that keep to these rules, and one draw needn't show every extreme that they name: `expert_ids`: each row names 8 different experts. Within the rows of one index of expert (aligned blocks of 128 rows) no expert is named by more than 32 rows, a bound that some block reaches.
All inputs are finite; a program needn't handle non-finite values.
Results may differ from a plain program's by a relative error of at most 0.035.
Values may be sent and summed in bfloat16 or wider, within the bound.
No kernel may reach another device: no remote copies, remote signals or barrier semaphores. Data moves between devices by JAX's collectives and lax.ppermute only.
A program may use at most 128 MiB of HBM per device.

v0:
```python
import jax
import jax.numpy as jnp
from jax import lax
from jax.sharding import PartitionSpec as P


def slot_tables(expert_ids, columns, per_device, capacity):
    flat_ids = expert_ids.reshape(-1)
    assign_count = flat_ids.shape[0]
    experts_all = columns * per_device
    onehot = (flat_ids[:, None] == jnp.arange(experts_all, dtype=jnp.int32)[None, :]).astype(
        jnp.int32
    )
    before = jnp.cumsum(onehot, axis=0) - onehot
    rank_in = jnp.sum(before * onehot, axis=1)
    slot_of = (flat_ids % per_device * columns + flat_ids // per_device) * capacity + rank_in
    slot_count = experts_all * capacity
    source = (
        jnp.full((slot_count,), assign_count, jnp.int32)
        .at[slot_of]
        .set(jnp.arange(assign_count, dtype=jnp.int32))
    )
    return (slot_of, source)


def run_groups(bundles, hidden_units):
    parties = lax.axis_size("dp")
    row_totals = [bundle[0].shape[0] * bundle[0].shape[1] for bundle in bundles]
    gate_part = jnp.concatenate(
        [
            jnp.einsum(
                "grd,gdf->grf", bundle[0], bundle[2], preferred_element_type=jnp.float32
            ).reshape(-1, hidden_units)
            for bundle in bundles
        ],
        axis=0,
    )
    up_part = jnp.concatenate(
        [
            jnp.einsum(
                "grd,gdf->grf", bundle[0], bundle[3], preferred_element_type=jnp.float32
            ).reshape(-1, hidden_units)
            for bundle in bundles
        ],
        axis=0,
    )
    total_rows = gate_part.shape[0]
    share_rows = total_rows // parties
    share_start = lax.axis_index("dp") * share_rows
    gate_pre, up_pre = (
        lax.psum(gate_part.astype(jnp.bfloat16), "dp").astype(jnp.float32),
        lax.psum(up_part.astype(jnp.bfloat16), "dp").astype(jnp.float32),
    )
    hidden = (jax.nn.silu(gate_pre) * up_pre).astype(jnp.bfloat16)
    gate_share = lax.dynamic_slice_in_dim(gate_pre, share_start, share_rows, 0)
    up_share = lax.dynamic_slice_in_dim(up_pre, share_start, share_rows, 0)
    hidden_part = jnp.concatenate(
        [
            jnp.einsum(
                "grd,gfd->grf", bundle[1], bundle[4], preferred_element_type=jnp.float32
            ).reshape(-1, hidden_units)
            for bundle in bundles
        ],
        axis=0,
    )
    hidden_grad = lax.psum_scatter(
        hidden_part.astype(jnp.bfloat16), "dp", scatter_dimension=0, tiled=True
    ).astype(jnp.float32)
    sigmoid_g = jax.nn.sigmoid(gate_share)
    gate_grad = (
        hidden_grad * up_share * sigmoid_g * (1.0 + gate_share * (1.0 - sigmoid_g))
    ).astype(jnp.bfloat16)
    up_grad = (hidden_grad * gate_share * sigmoid_g).astype(jnp.bfloat16)
    gate_rows, up_rows = (
        lax.all_gather(gate_grad, "dp", axis=0, tiled=True),
        lax.all_gather(up_grad, "dp", axis=0, tiled=True),
    )
    outputs = []
    offset = 0
    for bundle, row_total in zip(bundles, row_totals):
        piece_shape = (bundle[0].shape[0], bundle[0].shape[1], hidden_units)
        hidden_piece = hidden.reshape(piece_shape)
        gate_piece = gate_rows.reshape(piece_shape)
        up_piece = up_rows.reshape(piece_shape)
        offset = offset + row_total
        expert_out = jnp.einsum(
            "grf,gfd->grd", hidden_piece, bundle[4], preferred_element_type=jnp.float32
        ).astype(jnp.bfloat16)
        slot_grad = (
            jnp.einsum("grf,gdf->grd", gate_piece, bundle[2], preferred_element_type=jnp.float32)
            + jnp.einsum("grf,gdf->grd", up_piece, bundle[3], preferred_element_type=jnp.float32)
        ).astype(jnp.bfloat16)
        dw_gate = jnp.einsum(
            "grd,grf->gdf", bundle[0], gate_piece, preferred_element_type=jnp.float32
        )
        dw_up = jnp.einsum("grd,grf->gdf", bundle[0], up_piece, preferred_element_type=jnp.float32)
        dw_down = jnp.einsum(
            "grf,grd->gfd", hidden_piece, bundle[1], preferred_element_type=jnp.float32
        )
        outputs.append((expert_out, slot_grad, dw_gate, dw_up, dw_down))
    return outputs


def on_device(tokens, expert_ids, gate_prob, w_gate, w_up, w_down, grad_out):
    tok_rows, fanout = expert_ids.shape
    per_device, slice_width, hidden_units = w_gate.shape
    columns = lax.axis_size("expert")
    capacity = 2 * tok_rows * fanout // (per_device * columns)
    slot_count = per_device * columns * capacity
    assign_count = tok_rows * fanout
    slot_of, source = slot_tables(expert_ids, columns, per_device, capacity)
    filled = source < assign_count
    safe_src = jnp.minimum(source, assign_count - 1)
    tok_index = safe_src // fanout
    gate_flat = gate_prob.reshape(-1)
    token_buffer = jnp.where(filled[:, None], tokens[tok_index], jnp.zeros((), jnp.bfloat16))
    gate_slots = jnp.where(filled, gate_flat[safe_src], jnp.zeros((), jnp.float32))
    grad_buffer = (gate_slots[:, None] * grad_out[tok_index].astype(jnp.float32)).astype(
        jnp.bfloat16
    )
    layout = (per_device, columns, capacity, slice_width)
    sent_tokens, sent_grads = (
        lax.all_to_all(
            token_buffer.reshape(layout), "expert", split_axis=1, concat_axis=1, tiled=True
        ),
        lax.all_to_all(
            grad_buffer.reshape(layout), "expert", split_axis=1, concat_axis=1, tiled=True
        ),
    )
    bundles = [
        (
            sent_tokens.reshape(per_device, columns * capacity, slice_width),
            sent_grads.reshape(per_device, columns * capacity, slice_width),
            w_gate,
            w_up,
            w_down,
        )
    ]
    results = run_groups(bundles, hidden_units)
    expert_out = results[0][0].reshape(layout)
    slot_grad = results[0][1].reshape(layout)
    total_gate = results[0][2]
    total_up = results[0][3]
    total_down = results[0][4]
    grad_w_gate = total_gate.astype(jnp.bfloat16)
    grad_w_up = total_up.astype(jnp.bfloat16)
    grad_w_down = total_down.astype(jnp.bfloat16)
    back_out, back_grad = (
        lax.all_to_all(expert_out, "expert", split_axis=1, concat_axis=1, tiled=True),
        lax.all_to_all(slot_grad, "expert", split_axis=1, concat_axis=1, tiled=True),
    )
    out_rows = (
        back_out.reshape(slot_count, slice_width)[slot_of]
        .reshape(tok_rows, fanout, slice_width)
        .astype(jnp.float32)
    )
    grad_rows = (
        back_grad.reshape(slot_count, slice_width)[slot_of]
        .reshape(tok_rows, fanout, slice_width)
        .astype(jnp.float32)
    )
    mixed = jnp.sum(gate_prob[:, :, None] * out_rows, axis=1).astype(jnp.bfloat16)
    grad_tokens = jnp.sum(grad_rows, axis=1).astype(jnp.bfloat16)
    partial_dots = jnp.sum(out_rows * grad_out.astype(jnp.float32)[:, None, :], axis=2)
    grad_gate = lax.psum(partial_dots, "dp")
    return (mixed, grad_tokens, grad_gate, grad_w_gate, grad_w_up, grad_w_down)


def solution(mesh):
    return jax.shard_map(
        on_device,
        mesh=mesh,
        in_specs=(
            P("expert", "dp"),
            P("expert", None),
            P("expert", None),
            P("expert", "dp", None),
            P("expert", "dp", None),
            P("expert", None, "dp"),
            P("expert", "dp"),
        ),
        out_specs=(
            P("expert", "dp"),
            P("expert", "dp"),
            P("expert", None),
            P("expert", "dp", None),
            P("expert", "dp", None),
            P("expert", None, "dp"),
        ),
        check_vma=False,
    )
```

profile of v0, /device:TPU:32, one launch (start us, length us, event | category | flops | bytes accessed | tf_op | source)
XLA Modules:
  0.0 592.9 jit_solution(16468973395299543634)
XLA Ops:
  7.2 0.9 copy.47
  8.3 0.1 reshape.224
  8.4 0.8 copy.46
  9.2 0.1 reshape.230
  9.3 18.0 %reduce-window.6 = s32[64,8,128]{2,1,0:T(8,128)S(1)} reduce-window(s32[64,8,128]{2,1,0:T(8,128)S(1)} %fusion.11, s32[]{:T(128)} %constant.58.clone.1), window={size=1x1x128 pad=0_0x0_0x127_0}, to_apply=%region_0.0 | reduce-window | flops 8323072 | bytes 524292 | tf_op jit(solution)/shard_map/reduce-window
  27.3 0.1 slice.18
  27.5 0.1 copy.50
  27.7 0.1 broadcast_add_fusion
  28.0 4.3 scatter_custom_fusion
  32.4 8.6 %gather_fusion.2 = f32[2048]{0:T(1024)S(1)} fusion(f32[1024]{0:T(1024)S(1)} %reshape.230, s32[2048]{0:T(1024)S(1)} %get-tuple-element.26), kind=kCustom, calls=%fused_computation.2 | custom fusion | bytes 24576 | tf_op jit(solution)/shard_map/gather | solution.py:117
  41.1 7.5 %gather_fusion = bf16[2048,256]{1,0:T(8,128)(2,1)S(1)} fusion(bf16[128,256]{1,0:T(8,128)(2,1)S(1)} %copy-done.2, s32[2048]{0:T(1024)S(1)} %get-tuple-element.27), kind=kCustom, calls=%fused_computation | custom fusion | bytes 2105344 | tf_op jit(solution)/shard_map/gather | solution.py:116
  48.6 0.4 copy_select_fusion
  49.1 35.7 %all_to_all.20 = bf16[4,16,32,256]{3,2,0,1:T(8,128)(2,1)S(1)} all-to-all(bf16[4,16,32,256]{3,2,0,1:T(8,128)(2,1)S(1)} %copy_select_fusion), channel_id=1, replica_groups=mesh['dp'=16,'expert'=16] {'expert'}, dimensions={1} | all-to-all | bytes 2097152 | tf_op jit(solution)/shard_map/all_to_all | solution.py:123
  84.9 2.6 convolution_convert_fusion.1
  87.5 2.6 convolution_convert_fusion.2
  90.3 0.7 copy-done.1
  91.0 7.5 %gather_fusion.3 = bf16[2048,256]{1,0:T(8,128)(2,1)S(1)} fusion(bf16[128,256]{1,0:T(8,128)(2,1)S(1)} %copy-done.1, s32[2048]{0:T(1024)S(1)} %get-tuple-element.27), kind=kCustom, calls=%fused_computation.3 | custom fusion | bytes 2105344 | tf_op jit(solution)/shard_map/gather | solution.py:118
  98.5 0.3 fusion
  98.8 32.5 %all_to_all.21 = bf16[4,16,32,256]{3,2,0,1:T(8,128)(2,1)S(1)} all-to-all(bf16[4,16,32,256]{3,2,0,1:T(8,128)(2,1)S(1)} %fusion), channel_id=1, replica_groups=mesh['dp'=16,'expert'=16] {'expert'}, dimensions={1} | all-to-all | bytes 2097152 | tf_op jit(solution)/shard_map/all_to_all | solution.py:126
  131.4 2.7 convolution_convert_fusion
  134.2 139.9 %all-reduce.3.cloned.1.call-done = (bf16[2048,768]{1,0:T(8,128)(2,1)}, bf16[2048,768]{1,0:T(8,128)(2,1)}) async-done(((bf16[2048,768]{1,0:T(8,128)(2,1)}, bf16[2048,768]{1,0:T(8,128)(2,1)}), (bf16[2048,768]{1,0:T(8,128)(2,1)}, bf16[2048,768]{1,0:T(8,128)(2,1)})) %all-reduce.3.cloned.1.call-update) | async-done | bytes 6291472 | tf_op jit(solution)/shard_map/psum | solution.py:52
  274.1 5.2 convert_element_type.91
  279.3 3.1 convert_element_type.94
  282.4 79.0 %reduce-scatter.2.cloned.1.call-done = bf16[128,768]{1,0:T(8,128)(2,1)} async-done(((bf16[2048,768]{1,0:T(8,128)(2,1)}), bf16[128,768]{1,0:T(8,128)(2,1)}) %reduce-scatter.2.cloned.1.call-update) | async-done | bytes 196624 | tf_op jit(solution)/shard_map/reduce_scatter | solution.py:66
  361.5 2.1 fusion.7
  363.7 0.5 all-gather.5.cloned.1.call-update
  364.2 3.8 multiply_convert_fusion
  368.1 1.0 convolution_convert_fusion.6
  369.1 0.7 copy-done.7
  369.8 1.0 copy.55
  370.8 7.5 %all-to-all-start.1 = ((bf16[4,16,32,256]{3,2,0,1:T(8,128)(2,1)}), bf16[4,16,32,256]{3,2,0,1:T(8,128)(2,1)}, u32[]{:S(2)}, u32[]{:S(2)}) async-start(bf16[4,16,32,256]{3,2,0,1:T(8,128)(2,1)} %copy.55), calls=%async_computation.1 | async-start | bytes 2097152 | tf_op jit(solution)/shard_map/all_to_all | solution.py:149
  378.3 42.8 %all-gather.3.cloned.1.call-done = bf16[2048,768]{1,0:T(8,128)(2,1)} async-done(((bf16[128,768]{1,0:T(8,128)(2,1)}), bf16[2048,768]{1,0:T(8,128)(2,1)}) %all-gather.3.cloned.1.call-update) | async-done | bytes 3145744 | tf_op jit(solution)/shard_map/all_gather | solution.py:75
  421.1 4.7 fusion.20
  425.8 54.7 %all-gather.5.cloned.1.call-done = bf16[2048,768]{1,0:T(8,128)(2,1)} async-done(((bf16[128,768]{1,0:T(8,128)(2,1)}), bf16[2048,768]{1,0:T(8,128)(2,1)}) %all-gather.5.cloned.1.call-update) | async-done | bytes 3145744 | tf_op jit(solution)/shard_map/all_gather | solution.py:76
  480.5 4.0 add_convert_fusion
  484.5 1.1 copy.61
  485.6 7.5 %all-to-all-start.3 = ((bf16[4,16,32,256]{3,2,0,1:T(8,128)(2,1)}), bf16[4,16,32,256]{3,2,0,1:T(8,128)(2,1)}, u32[]{:S(2)}, u32[]{:S(2)}) async-start(bf16[4,16,32,256]{3,2,0,1:T(8,128)(2,1)} %copy.61), calls=%async_computation.4 | async-start | bytes 2097152 | tf_op jit(solution)/shard_map/all_to_all | solution.py:150
  493.1 4.3 convolution_convert_fusion.3
  497.4 1.3 copy.56
  498.7 3.9 gather_fusion.1
  502.7 1.1 fusion.2
  503.8 69.0 %psum.23 = f32[128,8]{1,0:T(8,128)S(1)} all-reduce(f32[128,8]{1,0:T(8,128)S(1)} %get-tuple-element.18), channel_id=1, replica_groups=mesh['dp'=16,'expert'=16] {'dp'}, use_global_device_ids=true, to_apply=%region_10.11 | all-reduce | flops 1024 | bytes 8192 | tf_op jit(solution)/shard_map/psum | solution.py:165
  572.8 0.7 copy.66
  573.4 4.5 convolution_convert_fusion.5
  578.0 2.2 convolution_convert_fusion.4
  580.2 1.3 copy.62
  581.5 3.9 gather_fusion.4
  585.4 1.0 bitcast_reduce_fusion
  (46 shorter events, 1.1 us)
Async XLA Ops:
  7.2 124.3 %copy-start = (bf16[4,768,256]{2,1,0:T(8,128)(2,1)S(1)}, bf16[4,768,256]{2,1,0:T(8,128)(2,1)}, u32[]{:S(2)}) copy-start(bf16[4,768,256]{2,1,0:T(8,128)(2,1)} %param.12) | copy-start | bytes 4718596
  7.2 266.9 %all-reduce.3.cloned.1.call-start = ((), (), s32[]{:S(2)}) async-start(), calls=%async_computation.8 | async-start | bytes 12582912 | tf_op jit(solution)/shard_map/psum | solution.py:52
  32.4 8.7 %copy-start.2 = (bf16[128,256]{1,0:T(8,128)(2,1)S(1)}, bf16[128,256]{1,0:T(8,128)(2,1)}, u32[]{:S(2)}) copy-start(bf16[128,256]{1,0:T(8,128)(2,1)} %param.7) | copy-start | bytes 196612
  48.6 36.3 %copy-start.9 = (bf16[4,256,768]{2,1,0:T(8,128)(2,1)S(1)}, bf16[4,256,768]{2,1,0:T(8,128)(2,1)}, u32[]{:S(2)}) copy-start(bf16[4,256,768]{2,1,0:T(8,128)(2,1)} %param.11) | copy-start | bytes 4718596
  84.8 5.3 copy-start.3
  84.8 2.7 copy-start.8
  90.2 0.8 copy-start.1
  90.2 271.3 %reduce-scatter.2.cloned.1.call-start = ((), (), s32[]{:S(2)}) async-start(), calls=%async_computation.5 | async-start | bytes 3342336 | tf_op jit(solution)/shard_map/reduce_scatter | solution.py:66
  134.2 287.0 %all-gather.3.cloned.1.call-start = ((), (), s32[]{:S(2)}) async-start(), calls=%async_computation.6 | async-start | bytes 3342336 | tf_op jit(solution)/shard_map/all_gather | solution.py:75
  274.1 5.2 copy-start.5
  363.6 116.8 %all-gather.5.cloned.1.call-start = ((), (), s32[]{:S(2)}) async-start(), calls=%async_computation.7 | async-start | bytes 3342336 | tf_op jit(solution)/shard_map/all_gather | solution.py:76
  368.1 1.7 copy-start.7
  370.8 114.8 %all-to-all-start.1 = ((bf16[4,16,32,256]{3,2,0,1:T(8,128)(2,1)}), bf16[4,16,32,256]{3,2,0,1:T(8,128)(2,1)}, u32[]{:S(2)}, u32[]{:S(2)}) async-start(bf16[4,16,32,256]{3,2,0,1:T(8,128)(2,1)} %copy.55), calls=%async_computation.1 | async-start | bytes 2097152 | tf_op jit(solution)/shard_map/all_to_all | solution.py:149
  485.6 94.6 %all-to-all-start.3 = ((bf16[4,16,32,256]{3,2,0,1:T(8,128)(2,1)}), bf16[4,16,32,256]{3,2,0,1:T(8,128)(2,1)}, u32[]{:S(2)}, u32[]{:S(2)}) async-start(bf16[4,16,32,256]{3,2,0,1:T(8,128)(2,1)} %copy.61), calls=%async_computation.4 | async-start | bytes 2097152 | tf_op jit(solution)/shard_map/all_to_all | solution.py:150
  503.8 74.2 %copy-start.4 = (bf16[4,16,32,256]{3,2,1,0:T(8,128)(2,1)S(1)}, bf16[4,16,32,256]{3,2,1,0:T(8,128)(2,1)}, u32[]{:S(2)}) copy-start(bf16[4,16,32,256]{3,2,1,0:T(8,128)(2,1)} %copy-done.3) | copy-start | bytes 3145732
  573.4 4.5 copy-start.6
Sparse Core Ops, SparseCore 0:
  90.3 183.7 all-reduce.2
  278.4 83.0 reduce-scatter.1
  364.2 56.9 all-gather.2
  424.2 56.2 all-gather.4
where the time goes:
time: 594 us; the launch traced here: 593 us
  waiting for transfers between devices  317 us (53%)
  blocking collectives  137 us (23%)
  local copies, waits for them, and re-layouts  45.3 us (8%)
  other arithmetic  35.5 us (6%)
  matrix products  28.7 us (5%)
  starting transfers between devices  15.2 us (3%)
  between operations  14.1 us (2%)
    psum x1, waiting for transfers between devices, run_groups(): lax.psum(up_part.astype(jnp.bfloat16), 'dp').astype(jnp.float32)  140 us
    reduce_scatter x1, waiting for transfers between devices, run_groups(): lax.psum_scatter(hidden_part.astype(jnp.bfloat16), 'dp', scatter_dimensio...  79 us
    psum x1, blocking collectives, on_device(): grad_gate = lax.psum(partial_dots, 'dp')  69 us
    all_gather x1, waiting for transfers between devices, run_groups(): lax.all_gather(up_grad, 'dp', axis=0, tiled=True)  54.7 us
    all_gather x1, waiting for transfers between devices, run_groups(): lax.all_gather(gate_grad, 'dp', axis=0, tiled=True)  42.8 us
    all_to_all x1, blocking collectives, on_device(): lax.all_to_all(token_buffer.reshape(layout), 'expert', split_axis=1, conc...  35.7 us
    all_to_all x1, blocking collectives, on_device(): lax.all_to_all(grad_buffer.reshape(layout), 'expert', split_axis=1, conca...  32.5 us
    another operation x3, other arithmetic  18.2 us
  transfers between devices with their start and end apart: 6, of which 4 were waited for; matrix products, arithmetic and copies ran while one was open for 9% of the time, Pallas kernels for 0%

commit v1 on v0

--- a/solution.py
+++ b/solution.py
@@ -73,7 +73,9 @@
     up_grad = (hidden_grad * gate_share * sigmoid_g).astype(jnp.bfloat16)
     gate_rows, up_rows = (
         lax.all_gather(gate_grad, "dp", axis=0, tiled=True),
-        lax.all_gather(up_grad, "dp", axis=0, tiled=True),
+        jnp.concatenate(
+            lax.all_to_all(jnp.stack([up_grad] * lax.axis_size("dp")), "dp", 0, 0), axis=0
+        ),
     )
     outputs = []
     offset = 0

time: 594 us -> 561 us (0.944)
  waiting for transfers between devices: 317 us -> 280 us
  starting transfers between devices: 15.2 us -> 21.7 us
    all_gather x1 -> x0, waiting for transfers between devices: 54.7 us -> none  [run_groups(): lax.all_gather(up_grad, 'dp', axis=0, tiled=True)]
    all_to_all x0 -> x1, waiting for transfers between devices: none -> 37.1 us  [run_groups(): lax.all_to_all(jnp.stack([up_grad] * lax.axis_size('dp')), 'dp', 0, 0)]
    all_gather x1, waiting for transfers between devices: 42.8 us -> 23.2 us  [run_groups(): lax.all_gather(gate_grad, 'dp', axis=0, tiled=True)]
where the time goes in v1:
time: 561 us
  waiting for transfers between devices  280 us (50%)
  blocking collectives  136 us (24%)
  local copies, waits for them, and re-layouts  47.3 us (8%)
  other arithmetic  35.4 us (6%)
  matrix products  26.3 us (5%)
  starting transfers between devices  21.7 us (4%)
  between operations  14.1 us (3%)
    psum x1, waiting for transfers between devices, run_groups(): lax.psum(up_part.astype(jnp.bfloat16), 'dp').astype(jnp.float32)  141 us
    reduce_scatter x1, waiting for transfers between devices, run_groups(): lax.psum_scatter(hidden_part.astype(jnp.bfloat16), 'dp', scatter_dimensio...  79 us
    psum x1, blocking collectives, on_device(): grad_gate = lax.psum(partial_dots, 'dp')  67.8 us
    all_to_all x1, waiting for transfers between devices, run_groups(): lax.all_to_all(jnp.stack([up_grad] * lax.axis_size('dp')), 'dp', 0, 0)  37.1 us
    all_to_all x1, blocking collectives, on_device(): lax.all_to_all(token_buffer.reshape(layout), 'expert', split_axis=1, conc...  35.7 us
    all_to_all x1, blocking collectives, on_device(): lax.all_to_all(grad_buffer.reshape(layout), 'expert', split_axis=1, conca...  32.5 us
    all_gather x1, waiting for transfers between devices, run_groups(): lax.all_gather(gate_grad, 'dp', axis=0, tiled=True)  23.2 us
    another operation x3, other arithmetic  18.2 us
  transfers between devices with their start and end apart: 6, of which 4 were waited for; matrix products, arithmetic and copies ran while one was open for 9% of the time, Pallas kernels for 0%

profile of v1, /device:TPU:32, one launch (start us, length us, event | category | flops | bytes accessed | tf_op | source)
XLA Modules:
  0.0 560.7 jit_solution(265368643715612180)
XLA Ops:
  7.2 0.9 copy.47
  8.3 0.1 reshape.223
  8.4 0.8 copy.46
  9.3 18.0 %reduce-window.6 = s32[64,8,128]{2,1,0:T(8,128)S(1)} reduce-window(s32[64,8,128]{2,1,0:T(8,128)S(1)} %fusion.11, s32[]{:T(128)} %constant.58.clone.1), window={size=1x1x128 pad=0_0x0_0x127_0}, to_apply=%region_0.0 | reduce-window | flops 8323072 | bytes 524292 | tf_op jit(solution)/shard_map/reduce-window
  27.3 0.1 slice.18
  27.5 0.1 copy.50
  27.7 0.1 broadcast_add_fusion
  28.0 4.3 scatter_custom_fusion
  32.4 8.6 %gather_fusion.2 = f32[2048]{0:T(1024)S(1)} fusion(f32[1024]{0:T(1024)S(1)} %reshape.229, s32[2048]{0:T(1024)S(1)} %get-tuple-element.26), kind=kCustom, calls=%fused_computation.2 | custom fusion | bytes 24576 | tf_op jit(solution)/shard_map/gather | solution.py:119
  41.1 7.5 %gather_fusion = bf16[2048,256]{1,0:T(8,128)(2,1)S(1)} fusion(bf16[128,256]{1,0:T(8,128)(2,1)S(1)} %copy-done.2, s32[2048]{0:T(1024)S(1)} %get-tuple-element.27), kind=kCustom, calls=%fused_computation | custom fusion | bytes 2105344 | tf_op jit(solution)/shard_map/gather | solution.py:118
  48.6 0.4 copy_select_fusion
  49.1 35.7 %all_to_all.25 = bf16[4,16,32,256]{3,2,0,1:T(8,128)(2,1)S(1)} all-to-all(bf16[4,16,32,256]{3,2,0,1:T(8,128)(2,1)S(1)} %copy_select_fusion), channel_id=1, replica_groups=mesh['dp'=16,'expert'=16] {'expert'}, dimensions={1} | all-to-all | bytes 2097152 | tf_op jit(solution)/shard_map/all_to_all | solution.py:125
  84.9 2.6 convolution_convert_fusion.1
  87.5 2.6 convolution_convert_fusion.2
  90.3 0.7 copy-done.1
  91.0 7.5 %gather_fusion.3 = bf16[2048,256]{1,0:T(8,128)(2,1)S(1)} fusion(bf16[128,256]{1,0:T(8,128)(2,1)S(1)} %copy-done.1, s32[2048]{0:T(1024)S(1)} %get-tuple-element.27), kind=kCustom, calls=%fused_computation.3 | custom fusion | bytes 2105344 | tf_op jit(solution)/shard_map/gather | solution.py:120
  98.5 0.3 fusion
  98.8 32.5 %all_to_all.26 = bf16[4,16,32,256]{3,2,0,1:T(8,128)(2,1)S(1)} all-to-all(bf16[4,16,32,256]{3,2,0,1:T(8,128)(2,1)S(1)} %fusion), channel_id=1, replica_groups=mesh['dp'=16,'expert'=16] {'expert'}, dimensions={1} | all-to-all | bytes 2097152 | tf_op jit(solution)/shard_map/all_to_all | solution.py:128
  131.4 2.7 convolution_convert_fusion
  134.2 140.5 %all-reduce.3.cloned.1.call-done = (bf16[2048,768]{1,0:T(8,128)(2,1)}, bf16[2048,768]{1,0:T(8,128)(2,1)}) async-done(((bf16[2048,768]{1,0:T(8,128)(2,1)}, bf16[2048,768]{1,0:T(8,128)(2,1)}), (bf16[2048,768]{1,0:T(8,128)(2,1)}, bf16[2048,768]{1,0:T(8,128)(2,1)})) %all-reduce.3.cloned.1.call-update) | async-done | bytes 6291472 | tf_op jit(solution)/shard_map/psum | solution.py:52
  274.8 5.2 convert_element_type.91
  279.9 3.1 convert_element_type.94
  283.1 79.0 %reduce-scatter.2.cloned.1.call-done = bf16[128,768]{1,0:T(8,128)(2,1)} async-done(((bf16[2048,768]{1,0:T(8,128)(2,1)}), bf16[128,768]{1,0:T(8,128)(2,1)}) %reduce-scatter.2.cloned.1.call-update) | async-done | bytes 196624 | tf_op jit(solution)/shard_map/reduce_scatter | solution.py:66
  362.1 2.1 fusion.7
  364.2 2.0 stack.2
  366.2 4.5 all-to-all-start.3
  370.7 3.8 multiply_convert_fusion
  374.6 1.0 convolution_convert_fusion.6
  375.5 0.6 copy-done.7
  376.2 1.0 copy.55
  377.2 37.1 %all-to-all-done.3 = bf16[16,128,768]{2,1,0:T(8,128)(2,1)} async-done(((bf16[16,128,768]{2,1,0:T(8,128)(2,1)}), bf16[16,128,768]{2,1,0:T(8,128)(2,1)}, u32[]{:S(2)}, u32[]{:S(2)}) %all-to-all-start.3) | async-done | bytes 3145760 | tf_op jit(solution)/shard_map/all_to_all | solution.py:77
  414.3 7.8 %all-to-all-start.1 = ((bf16[4,16,32,256]{3,2,0,1:T(8,128)(2,1)}), bf16[4,16,32,256]{3,2,0,1:T(8,128)(2,1)}, u32[]{:S(2)}, u32[]{:S(2)}) async-start(bf16[4,16,32,256]{3,2,0,1:T(8,128)(2,1)} %copy.55), calls=%async_computation.1 | async-start | bytes 2097152 | tf_op jit(solution)/shard_map/all_to_all | solution.py:151
  422.1 23.2 %all-gather.2.cloned.1.call-done = bf16[2048,768]{1,0:T(8,128)(2,1)} async-done(((bf16[128,768]{1,0:T(8,128)(2,1)}), bf16[2048,768]{1,0:T(8,128)(2,1)}) %all-gather.2.cloned.1.call-update) | async-done | bytes 3145744 | tf_op jit(solution)/shard_map/all_gather | solution.py:75
  445.3 3.5 fusion.20
  448.8 2.9 add_convert_fusion
  451.7 1.1 copy.61
  452.8 9.2 %all-to-all-start.4 = ((bf16[4,16,32,256]{3,2,0,1:T(8,128)(2,1)}), bf16[4,16,32,256]{3,2,0,1:T(8,128)(2,1)}, u32[]{:S(2)}, u32[]{:S(2)}) async-start(bf16[4,16,32,256]{3,2,0,1:T(8,128)(2,1)} %copy.61), calls=%async_computation.5 | async-start | bytes 2097152 | tf_op jit(solution)/shard_map/all_to_all | solution.py:152
  462.1 4.3 convolution_convert_fusion.3
  466.4 1.3 copy.56
  467.7 3.9 gather_fusion.1
  471.6 1.1 fusion.2
  472.8 67.8 %psum.23 = f32[128,8]{1,0:T(8,128)S(1)} all-reduce(f32[128,8]{1,0:T(8,128)S(1)} %get-tuple-element.18), channel_id=1, replica_groups=mesh['dp'=16,'expert'=16] {'dp'}, use_global_device_ids=true, to_apply=%region_10.11 | all-reduce | flops 1024 | bytes 8192 | tf_op jit(solution)/shard_map/psum | solution.py:167
  540.5 0.7 copy.66
  541.2 4.5 convolution_convert_fusion.4
  545.7 2.2 convolution_convert_fusion.5
  547.9 1.3 copy.62
  549.2 3.9 gather_fusion.4
  553.2 1.0 bitcast_reduce_fusion
  (48 shorter events, 1.1 us)
Async XLA Ops:
  7.2 124.3 %copy-start = (bf16[4,768,256]{2,1,0:T(8,128)(2,1)S(1)}, bf16[4,768,256]{2,1,0:T(8,128)(2,1)}, u32[]{:S(2)}) copy-start(bf16[4,768,256]{2,1,0:T(8,128)(2,1)} %param.12) | copy-start | bytes 4718596
  7.2 267.6 %all-reduce.3.cloned.1.call-start = ((), (), s32[]{:S(2)}) async-start(), calls=%async_computation.8 | async-start | bytes 12582912 | tf_op jit(solution)/shard_map/psum | solution.py:52
  32.4 8.7 %copy-start.2 = (bf16[128,256]{1,0:T(8,128)(2,1)S(1)}, bf16[128,256]{1,0:T(8,128)(2,1)}, u32[]{:S(2)}) copy-start(bf16[128,256]{1,0:T(8,128)(2,1)} %param.7) | copy-start | bytes 196612
  48.6 36.3 %copy-start.9 = (bf16[4,256,768]{2,1,0:T(8,128)(2,1)S(1)}, bf16[4,256,768]{2,1,0:T(8,128)(2,1)}, u32[]{:S(2)}) copy-start(bf16[4,256,768]{2,1,0:T(8,128)(2,1)} %param.11) | copy-start | bytes 4718596
  84.8 5.3 copy-start.3
  84.8 2.7 copy-start.8
  90.2 0.8 copy-start.1
  90.2 271.9 %reduce-scatter.2.cloned.1.call-start = ((), (), s32[]{:S(2)}) async-start(), calls=%async_computation.6 | async-start | bytes 3342336 | tf_op jit(solution)/shard_map/reduce_scatter | solution.py:66
  134.2 311.2 %all-gather.2.cloned.1.call-start = ((), (), s32[]{:S(2)}) async-start(), calls=%async_computation.7 | async-start | bytes 3342336 | tf_op jit(solution)/shard_map/all_gather | solution.py:75
  274.7 5.2 copy-start.5
  366.2 48.1 %all-to-all-start.3 = ((bf16[16,128,768]{2,1,0:T(8,128)(2,1)}), bf16[16,128,768]{2,1,0:T(8,128)(2,1)}, u32[]{:S(2)}, u32[]{:S(2)}) async-start(bf16[16,128,768]{2,1,0:T(8,128)(2,1)} %stack.2), calls=%async_computation.4 | async-start | bytes 6291456 | tf_op jit(solution)/shard_map/all_to_all | solution.py:77
  374.5 1.6 copy-start.7
  414.3 38.5 %all-to-all-start.1 = ((bf16[4,16,32,256]{3,2,0,1:T(8,128)(2,1)}), bf16[4,16,32,256]{3,2,0,1:T(8,128)(2,1)}, u32[]{:S(2)}, u32[]{:S(2)}) async-start(bf16[4,16,32,256]{3,2,0,1:T(8,128)(2,1)} %copy.55), calls=%async_computation.1 | async-start | bytes 2097152 | tf_op jit(solution)/shard_map/all_to_all | solution.py:151
  445.3 3.5 copy-start.10
  452.8 95.1 %all-to-all-start.4 = ((bf16[4,16,32,256]{3,2,0,1:T(8,128)(2,1)}), bf16[4,16,32,256]{3,2,0,1:T(8,128)(2,1)}, u32[]{:S(2)}, u32[]{:S(2)}) async-start(bf16[4,16,32,256]{3,2,0,1:T(8,128)(2,1)} %copy.61), calls=%async_computation.5 | async-start | bytes 2097152 | tf_op jit(solution)/shard_map/all_to_all | solution.py:152
  472.8 73.0 %copy-start.4 = (bf16[4,16,32,256]{3,2,1,0:T(8,128)(2,1)S(1)}, bf16[4,16,32,256]{3,2,1,0:T(8,128)(2,1)}, u32[]{:S(2)}) copy-start(bf16[4,16,32,256]{3,2,1,0:T(8,128)(2,1)} %copy-done.3) | copy-start | bytes 3145732
  541.2 4.5 copy-start.6
Sparse Core Ops, SparseCore 0:
  90.3 184.3 all-reduce.2
  279.1 83.0 reduce-scatter.1
  365.4 79.9 all-gather.1
